TPU v7x, 512 devices: a whole 4x8x8 slice. The times are simulated.
512 devices in a mesh: member: 8 (over y_hi, x), lat: 64 (over y_lo, z, core).
Axes of the slice: x: 4, y: 8 (y_hi: 2, y_lo: 4; y = y_hi * 4 + y_lo), z: 8, core: 2. Of those that a mesh axis runs over, the one named last changes fastest.
Arguments:
- atmosphere: float32 [2, 16, 8, 384, 1536], P(None, 'member', None, 'lat'), may hold values from -4 to 4
- ocean_state: float32 [2, 384, 1536], P(None, 'lat', 'member'), may hold values from -4 to 4
- viscosity: float32 [384, 1536], P('lat', 'member'), may hold values from 0.02 to 0.2
- sea_mask: int32 [384, 1536], P('lat'), may hold values 0 or 1
- parameter_index: int32 [16], P('member'), may hold values from 0 to 31
- parameter_table: float32 [32, 3], replicated, may hold values from 0.1 to 0.3
- level_mix: float32 [8, 8], replicated, may hold values from -0.5 to 0.5
Outputs:
- atmos_out: float32 [2, 16, 8, 384, 1536], P(None, 'member', None, 'lat')
- ocean_out: float32 [2, 384, 1536], P(None, 'lat', 'member')
All inputs are finite; a program needn't handle non-finite values. No bound on the sum of `sea_mask` on one device may be relied on, other than what follows from the above.
Results may differ from a plain program's by a relative error of at most 0.00011.
Values sent between devices are 32-bit elements; how exact they have to be, the bound alone decides.
A program may use at most 64 MiB of HBM per device.

v0:
```python
import jax
import jax.numpy as jnp
from jax import lax
from jax.sharding import PartitionSpec as P

ASTEPS = 3
OSTEPS = 2
COUPLE = 2
ADVECTION = 0.1
OCEAN_GAIN = 0.5
OCEAN_DIFFUSION = 0.15


def with_halo(block, sides, width, periodic):
    for axis, dim in sides:
        count = lax.axis_size(axis)
        forward = [(i, i + 1) for i in range(count - 1)]
        if periodic:
            forward.append((count - 1, 0))
        backward = [(target, source) for source, target in forward]
        low = lax.ppermute(
            lax.slice_in_dim(block, block.shape[dim] - width, None, axis=dim), axis, forward
        )
        high = lax.ppermute(lax.slice_in_dim(block, 0, width, axis=dim), axis, backward)
        block = jnp.concatenate([low, block, high], axis=dim)
    return block


def lookup(parameter_index, parameter_table):
    onehot = (
        parameter_index[:, None] == jnp.arange(parameter_table.shape[0], dtype=jnp.int32)[None, :]
    ).astype(jnp.float32)
    picked = jnp.dot(
        onehot, parameter_table, precision=lax.Precision.HIGHEST, preferred_element_type=jnp.float32
    )
    return (0.6 * picked[:, 0], 2.0 * jnp.transpose(picked[:, 1:3]))


def atmos_step(padded_rows, surface, diffusivity, exchange, level_mix):
    centre = padded_rows[:, :, :, 1:-1, :]
    northern = padded_rows[:, :, :, 2:, :]
    southern = padded_rows[:, :, :, :-2, :]
    eastern = jnp.roll(centre, -1, axis=4)
    western = jnp.roll(centre, 1, axis=4)
    laplace = eastern + western + northern + southern - 4.0 * centre
    zonal_wind = centre[1]
    advected = (
        centre
        - ADVECTION * zonal_wind[None] * (eastern - western) * 0.5
        + diffusivity[None, :, None, None, None] * laplace
    )
    mixed_state = advected + jnp.einsum(
        "kl,fmlrn->fmkrn", level_mix, advected, precision=lax.Precision.HIGHEST
    )
    bottom = mixed_state[:, :, 0] + exchange[:, :, None, None] * (
        surface[:, None] - mixed_state[:, :, 0]
    )
    return mixed_state.at[:, :, 0].set(bottom)


def atmos_window(atmos_state, surface, diffusivity, exchange, level_mix):
    for substep in range(ASTEPS):
        padded_rows = with_halo(atmos_state, (("lat", 3),), 1, False)
        atmos_state = atmos_step(padded_rows, surface, diffusivity, exchange, level_mix)
    return atmos_state


def ocean_step(ocean, forcing, ocean_rate, ocean_mask):
    padded_ocean = with_halo(ocean, (("lat", 1),), 1, False)
    columns = with_halo(ocean, (("member", 2),), 1, True)
    eastern = columns[:, :, 2:]
    western = columns[:, :, :-2]
    laplace = padded_ocean[:, 2:] + padded_ocean[:, :-2] + eastern + western - 4.0 * ocean
    return ocean + ocean_mask[None] * (OCEAN_GAIN * forcing + ocean_rate * laplace)


def body(atmosphere, ocean_state, viscosity, sea_mask, parameter_index, parameter_table, level_mix):
    local_members = atmosphere.shape[1]
    tile_width = ocean_state.shape[2]
    members = local_members * lax.axis_size("member")
    diffusivity, exchange = lookup(parameter_index, parameter_table)
    full_mask = sea_mask.astype(jnp.float32)
    tile_start = lax.axis_index("member") * tile_width
    ocean = ocean_state
    ocean_mask = lax.dynamic_slice_in_dim(full_mask, tile_start, tile_width, 1)
    ocean_rate = jnp.stack([jnp.full_like(viscosity, OCEAN_DIFFUSION), viscosity])
    atmos_state = atmosphere
    for coupling in range(COUPLE):
        surface = lax.all_gather(ocean, "member", axis=2, tiled=True)
        atmos_state = atmos_window(atmos_state, surface, diffusivity, exchange, level_mix)
        flux_terms = jnp.sum(
            exchange[:, :, None, None] * (atmos_state[:, :, 0] - surface[:, None]), axis=1
        )
        forcing = lax.psum_scatter(flux_terms, "member", scatter_dimension=2, tiled=True) / members
        for substep in range(OSTEPS):
            ocean = ocean_step(ocean, forcing, ocean_rate, ocean_mask)
    return (atmos_state, ocean)


def solution(mesh):
    return jax.shard_map(
        body,
        mesh=mesh,
        in_specs=(
            P(None, "member", None, "lat", None),
            P(None, "lat", "member"),
            P("lat", "member"),
            P("lat", None),
            P("member"),
            P(),
            P(),
        ),
        out_specs=(P(None, "member", None, "lat", None), P(None, "lat", "member")),
        check_vma=False,
    )
```

profile of v0, /device:TPU:48, one launch (start us, length us, event | category | flops | bytes accessed | tf_op | source)
XLA Modules:
  0.0 473.0 jit_solution(4835626749836713685)
XLA Ops:
  7.2 1.1 fusion.208
  8.3 11.2 %collective-permute-start = (f32[2,2,8,1,1536]{4,2,3,1,0:T(8,128)S(1)}, f32[2,2,8,1,1536]{4,2,3,1,0:T(8,128)}, u32[]{:S(2)}, u32[]{:S(2)}) collective-permute-start(f32[2,2,8,1,1536]{4,2,3,1,0:T(8,128)S(1)} %get-tuple-element.118), channel_id=1, source_target_pairs={{1,0},{2,1},{3,2},{4,3},{5,4},{6,5},{7,6},{8,7},{9,8},{10,9},{11,1... | collective-permute-start | bytes 589832 | tf_op jit(solution)/shard_map/ppermute | solution.py:24
  19.5 1.9 collective-permute-start.1
  22.8 5.1 %collective-permute-start.10 = (f32[2,6,1]{2,1,0:T(8,128)}, f32[2,6,1]{2,1,0:T(8,128)}, u32[]{:S(2)}, u32[]{:S(2)}) collective-permute-start(f32[2,6,1]{2,1,0:T(8,128)} %get-tuple-element.132), channel_id=1, source_target_pairs={{64,0},{128,64},{192,128},{256,192},{320,256},{384,320},{448,384},... | collective-permute-start | bytes 152 | tf_op jit(solution)/shard_map/ppermute | solution.py:24
  27.9 1.9 collective-permute-start.11
  31.1 5.6 %collective-permute-start.8 = (f32[2,1,192]{2,1,0:T(1,128)}, f32[2,1,192]{2,1,0:T(1,128)}, u32[]{:S(2)}, u32[]{:S(2)}) collective-permute-start(f32[2,1,192]{2,1,0:T(1,128)} %copy.68), channel_id=1, source_target_pairs={{1,0},{2,1},{3,2},{4,3},{5,4},{6,5},{7,6},{8,7},{9,8},{10,9},{11,1... | collective-permute-start | bytes 4616 | tf_op jit(solution)/shard_map/ppermute | solution.py:24
  36.7 3.5 fusion.206
  40.2 0.9 multiply_bitcast_fusion
  42.3 50.8 %all_gather.6 = f32[2,6,1536]{1,0,2:T(2,128)S(1)} all-gather(f32[2,6,192]{1,0,2:T(2,128)S(1)} %copy.63), channel_id=1, replica_groups=mesh['member'=8,'lat'=64] {'member'}, dimensions={2}, use_global_device_ids=true | all-gather | bytes 82944 | tf_op jit(solution)/shard_map/all_gather | solution.py:89
  93.1 1.7 copy.64
  96.3 5.4 %fusion.5 = f32[2,2,8,6,1536]{4,2,3,1,0:T(8,128)S(1)} fusion(f32[2,2,8,6,1536]{4,2,3,1,0:T(8,128)S(1)} %copy-done.1, f32[2,2,8,1,1536]{4,2,3,1,0:T(8,128)} %collective-permute-done.1, f32[2,2,8,1,1536]{4,2,3,1,0:T(8,128)} %collective-permute-done, f32[2,2,8,6,1535]{4,2,3,1,0:T(8,128)} %get-tuple-element.115, f32[2,2,8,6,1]{4,2,3,1,0:T(8,128)S(1)} %get-tuple-element.117, ...), kind=kOutput, calls=%fused_computation.11 | convolution fusion | flops 37453824 | bytes 5701896 | tf_op jit(solution)/shard_map/kl,fmlrn->fmkrn/dot_general | solution.py:52
  102.0 0.9 scatter.20
  103.4 1.9 collective-permute-start.2
  105.3 2.4 collective-permute-start.3
  108.5 5.9 %collective-permute-done.3 = f32[2,2,8,1,1536]{4,2,3,1,0:T(8,128)S(1)} collective-permute-done((f32[2,2,8,1,1536]{4,2,3,1,0:T(8,128)S(1)}, f32[2,2,8,1,1536]{4,2,3,1,0:T(8,128)S(1)}, u32[]{:S(2)}, u32[]{:S(2)}) %collective-permute-start.3) | collective-permute-done | bytes 196640 | tf_op jit(solution)/shard_map/ppermute | solution.py:21
  114.4 2.6 fusion.4
  117.4 0.9 scatter.21
  118.8 1.9 collective-permute-start.4
  120.7 2.4 collective-permute-start.5
  123.9 1.9 collective-permute-start.9
  125.8 4.0 collective-permute-done.5
  129.8 2.6 fusion.3
  132.8 0.9 scatter.24
  133.7 1.8 fusion.197
  136.2 0.9 fusion.98
  137.5 0.8 copy.84
  138.3 1.8 reshape.255
  140.9 1.9 collective-permute-start.6
  142.8 82.0 %reduce-scatter.7.cloned.1.call-done = f32[192,12]{1,0:T(8,128)} async-done(((f32[1536,12]{1,0:T(8,128)}), f32[192,12]{1,0:T(8,128)}) %reduce-scatter.7.cloned.1.call-update) | async-done | bytes 9232
  224.8 1.0 reshape.256
  226.0 1.9 collective-permute-start.7
  228.8 5.8 %collective-permute-start.12 = (f32[2,1,192]{2,1,0:T(1,128)S(1)}, f32[2,1,192]{2,1,0:T(1,128)S(1)}, u32[]{:S(2)}, u32[]{:S(2)}) collective-permute-start(f32[2,1,192]{2,1,0:T(1,128)S(1)} %get-tuple-element.128), channel_id=1, source_target_pairs={{1,0},{2,1},{3,2},{4,3},{5,4},{6,5},{7,6},{8,7},{9,8},{10,9},{11,1... | collective-permute-start | bytes 4616 | tf_op jit(solution)/shard_map/ppermute | solution.py:24
  234.6 1.9 collective-permute-start.13
  236.6 6.6 %collective-permute-start.14 = (f32[2,6,1]{2,1,0:T(8,128)S(1)}, f32[2,6,1]{2,1,0:T(8,128)S(1)}, u32[]{:S(2)}, u32[]{:S(2)}) collective-permute-start(f32[2,6,1]{2,1,0:T(8,128)S(1)} %get-tuple-element.130), channel_id=1, source_target_pairs={{64,0},{128,64},{192,128},{256,192},{320,256},{384,320},{448,384},... | collective-permute-start | bytes 152 | tf_op jit(solution)/shard_map/ppermute | solution.py:24
  243.2 1.3 collective-permute-done.14
  244.5 2.1 collective-permute-start.15
  246.6 9.9 %collective-permute-done.15 = f32[2,6,1]{2,1,0:T(8,128)S(1)} collective-permute-done((f32[2,6,1]{2,1,0:T(8,128)S(1)}, f32[2,6,1]{2,1,0:T(8,128)S(1)}, u32[]{:S(2)}, u32[]{:S(2)}) %collective-permute-start.15) | collective-permute-done | bytes 80 | tf_op jit(solution)/shard_map/ppermute | solution.py:21
  256.8 51.3 %all_gather.7 = f32[2,6,1536]{1,0,2:T(2,128)S(1)} all-gather(f32[2,6,192]{1,0,2:T(2,128)S(1)} %copy.78), channel_id=1, replica_groups=mesh['member'=8,'lat'=64] {'member'}, dimensions={2}, use_global_device_ids=true | all-gather | bytes 82944 | tf_op jit(solution)/shard_map/all_gather | solution.py:89
  308.8 1.9 collective-permute-start.20
  310.8 2.4 collective-permute-start.21
  313.2 5.2 %fusion.2 = f32[2,2,8,6,1536]{4,2,3,1,0:T(8,128)S(1)} fusion(f32[2,2,8,6,1536]{4,2,3,1,0:T(8,128)S(1)} %scatter.24, f32[2,2,8,1,1536]{4,2,3,1,0:T(8,128)} %collective-permute-done.7, f32[2,2,8,1,1536]{4,2,3,1,0:T(8,128)} %collective-permute-done.6, f32[2,2,8,6,1535]{4,2,3,1,0:T(8,128)} %get-tuple-element.97, f32[2,2,8,6,1]{4,2,3,1,0:T(8,128)} %get-tuple-element.99, ...), kind=kOutput, calls=%fused_computation.5 | convolution fusion | flops 37453824 | bytes 5701896 | tf_op jit(solution)/shard_map/kl,fmlrn->fmkrn/dot_general | solution.py:52
  318.7 0.9 scatter.25
  320.1 5.3 %collective-permute-start.16 = (f32[2,2,8,1,1536]{4,2,3,1,0:T(8,128)S(1)}, f32[2,2,8,1,1536]{4,2,3,1,0:T(8,128)S(1)}, u32[]{:S(2)}, u32[]{:S(2)}) collective-permute-start(f32[2,2,8,1,1536]{4,2,3,1,0:T(8,128)S(1)} %get-tuple-element.92), channel_id=1, source_target_pairs={{1,0},{2,1},{3,2},{4,3},{5,4},{6,5},{7,6},{8,7},{9,8},{10,9},{11,1... | collective-permute-start | bytes 589832 | tf_op jit(solution)/shard_map/ppermute | solution.py:24
  325.4 1.9 collective-permute-start.17
  327.4 1.1 collective-permute-done.16
  328.5 5.9 %collective-permute-done.17 = f32[2,2,8,1,1536]{4,2,3,1,0:T(8,128)S(1)} collective-permute-done((f32[2,2,8,1,1536]{4,2,3,1,0:T(8,128)S(1)}, f32[2,2,8,1,1536]{4,2,3,1,0:T(8,128)S(1)}, u32[]{:S(2)}, u32[]{:S(2)}) %collective-permute-start.17) | collective-permute-done | bytes 196640 | tf_op jit(solution)/shard_map/ppermute | solution.py:21
  334.5 2.6 fusion.1
  337.4 0.9 scatter.26
  338.8 1.9 collective-permute-start.18
  340.7 2.4 collective-permute-start.19
  343.9 5.9 %collective-permute-done.19 = f32[2,2,8,1,1536]{4,2,3,1,0:T(8,128)S(1)} collective-permute-done((f32[2,2,8,1,1536]{4,2,3,1,0:T(8,128)S(1)}, f32[2,2,8,1,1536]{4,2,3,1,0:T(8,128)S(1)}, u32[]{:S(2)}, u32[]{:S(2)}) %collective-permute-start.19) | collective-permute-done | bytes 196640 | tf_op jit(solution)/shard_map/ppermute | solution.py:21
  349.8 2.6 fusion
  353.1 0.8 copy.86
  354.0 1.8 reshape.257
  355.9 1.9 collective-permute-start.22
  357.8 3.9 collective-permute-start.23
  361.7 0.9 scatter.29
  362.6 76.5 %reduce-scatter.9.cloned.1.call-done = f32[192,12]{1,0:T(8,128)} async-done(((f32[1536,12]{1,0:T(8,128)}), f32[192,12]{1,0:T(8,128)}) %reduce-scatter.9.cloned.1.call-update) | async-done | bytes 9232
  439.1 1.0 reshape.258
  440.4 3.5 collective-permute-start.24
  443.9 1.9 collective-permute-start.25
  445.9 8.0 %collective-permute-start.26 = (f32[2,6,1]{2,1,0:T(8,128)S(1)}, f32[2,6,1]{2,1,0:T(8,128)S(1)}, u32[]{:S(2)}, u32[]{:S(2)}) collective-permute-start(f32[2,6,1]{2,1,0:T(8,128)S(1)} %get-tuple-element.122), channel_id=1, source_target_pairs={{64,0},{128,64},{192,128},{256,192},{320,256},{384,320},{448,384},... | collective-permute-start | bytes 152 | tf_op jit(solution)/shard_map/ppermute | solution.py:24
  453.9 1.9 collective-permute-start.27
  455.9 9.6 %collective-permute-done.27 = f32[2,6,1]{2,1,0:T(8,128)S(1)} collective-permute-done((f32[2,6,1]{2,1,0:T(8,128)S(1)}, f32[2,6,1]{2,1,0:T(8,128)S(1)}, u32[]{:S(2)}, u32[]{:S(2)}) %collective-permute-start.27) | collective-permute-done | bytes 80 | tf_op jit(solution)/shard_map/ppermute | solution.py:21
  (111 shorter events, 17.1 us)
Async XLA Ops:
  7.2 89.1 %copy-start = (f32[8,8]{1,0:T(8,128)S(1)}, f32[8,8]{1,0:T(8,128)}, u32[]{:S(2)}) copy-start(f32[8,8]{1,0:T(8,128)} %param.25) | copy-start | bytes 772
  7.2 217.7 %reduce-scatter.7.cloned.1.call-start = ((), (), s32[]{:S(2)}) async-start(), calls=%async_computation.2 | async-start | bytes 884736
  8.3 87.9 %collective-permute-start = (f32[2,2,8,1,1536]{4,2,3,1,0:T(8,128)S(1)}, f32[2,2,8,1,1536]{4,2,3,1,0:T(8,128)}, u32[]{:S(2)}, u32[]{:S(2)}) collective-permute-start(f32[2,2,8,1,1536]{4,2,3,1,0:T(8,128)S(1)} %get-tuple-element.118), channel_id=1, source_target_pairs={{1,0},{2,1},{3,2},{4,3},{5,4},{6,5},{7,6},{8,7},{9,8},{10,9},{11,1... | collective-permute-start | bytes 589832 | tf_op jit(solution)/shard_map/ppermute | solution.py:24
  19.5 76.8 %collective-permute-start.1 = (f32[2,2,8,1,1536]{4,2,3,1,0:T(8,128)S(1)}, f32[2,2,8,1,1536]{4,2,3,1,0:T(8,128)}, u32[]{:S(2)}, u32[]{:S(2)}) collective-permute-start(f32[2,2,8,1,1536]{4,2,3,1,0:T(8,128)S(1)} %get-tuple-element.119), channel_id=1, source_target_pairs={{0,1},{1,2},{2,3},{3,4},{4,5},{5,6},{6,7},{7,8},{8,9},{9,10},{10,1... | collective-permute-start | bytes 589832 | tf_op jit(solution)/shard_map/ppermute | solution.py:21
  22.1 8.4 %copy-start.6 = (f32[2,6,192]{2,1,0:T(8,128)}, f32[2,6,192]{2,1,0:T(8,128)S(1)}, u32[]{:S(2)}) copy-start(f32[2,6,192]{2,1,0:T(8,128)S(1)} %copy.77) | copy-start | bytes 27652
  22.8 203.2 %collective-permute-start.10 = (f32[2,6,1]{2,1,0:T(8,128)}, f32[2,6,1]{2,1,0:T(8,128)}, u32[]{:S(2)}, u32[]{:S(2)}) collective-permute-start(f32[2,6,1]{2,1,0:T(8,128)} %get-tuple-element.132), channel_id=1, source_target_pairs={{64,0},{128,64},{192,128},{256,192},{320,256},{384,320},{448,384},... | collective-permute-start | bytes 152 | tf_op jit(solution)/shard_map/ppermute | solution.py:24
  27.9 200.1 %collective-permute-start.11 = (f32[2,6,1]{2,1,0:T(8,128)}, f32[2,6,1]{2,1,0:T(8,128)}, u32[]{:S(2)}, u32[]{:S(2)}) collective-permute-start(f32[2,6,1]{2,1,0:T(8,128)} %get-tuple-element.133), channel_id=1, source_target_pairs={{0,64},{64,128},{128,192},{192,256},{256,320},{320,384},{384,448},... | collective-permute-start | bytes 152 | tf_op jit(solution)/shard_map/ppermute | solution.py:21
  31.1 9.1 %copy-start.1 = (f32[2,2,8,6,1536]{4,2,3,1,0:T(8,128)S(1)}, f32[2,2,8,6,1536]{4,2,3,1,0:T(8,128)}, u32[]{:S(2)}) copy-start(f32[2,2,8,6,1536]{4,2,3,1,0:T(8,128)} %param.19) | copy-start | bytes 3538948
  31.1 10.0 %copy-start.12 = (f32[32,3]{0,1:T(4,128)S(1)}, f32[32,3]{0,1:T(4,128)}, u32[]{:S(2)}) copy-start(f32[32,3]{0,1:T(4,128)} %param.24) | copy-start | bytes 1156
  31.1 10.0 %copy-start.13 = (s32[2]{0:T(128)S(1)}, s32[2]{0:T(128)}, u32[]{:S(2)}) copy-start(s32[2]{0:T(128)} %param.23) | copy-start | bytes 28
  31.1 196.8 %collective-permute-start.8 = (f32[2,1,192]{2,1,0:T(1,128)}, f32[2,1,192]{2,1,0:T(1,128)}, u32[]{:S(2)}, u32[]{:S(2)}) collective-permute-start(f32[2,1,192]{2,1,0:T(1,128)} %copy.68), channel_id=1, source_target_pairs={{1,0},{2,1},{3,2},{4,3},{5,4},{6,5},{7,6},{8,7},{9,8},{10,9},{11,1... | collective-permute-start | bytes 4616 | tf_op jit(solution)/shard_map/ppermute | solution.py:24
  40.2 1.9 copy-start.9
  96.3 5.4 %copy-start.2 = (f32[2,6,1536]{2,1,0:T(8,128)S(1)}, f32[2,6,1536]{2,1,0:T(8,128)}, u32[]{:S(2)}) copy-start(f32[2,6,1536]{2,1,0:T(8,128)} %copy.64) | copy-start | bytes 221188
  103.3 11.1 %copy-start.14 = (f32[2]{0:T(128)S(1)}, f32[2]{0:T(128)}, u32[]{:S(2)}) copy-start(f32[2]{0:T(128)} %multiply_reduce_fusion) | copy-start | bytes 28
  103.4 5.1 %collective-permute-start.2 = (f32[2,2,8,1,1536]{4,2,3,1,0:T(8,128)S(1)}, f32[2,2,8,1,1536]{4,2,3,1,0:T(8,128)S(1)}, u32[]{:S(2)}, u32[]{:S(2)}) collective-permute-start(f32[2,2,8,1,1536]{4,2,3,1,0:T(8,128)S(1)} %get-tuple-element.112), channel_id=1, source_target_pairs={{1,0},{2,1},{3,2},{4,3},{5,4},{6,5},{7,6},{8,7},{9,8},{10,9},{11,1... | collective-permute-start | bytes 589832 | tf_op jit(solution)/shard_map/ppermute | solution.py:24
  105.3 9.1 %collective-permute-start.3 = (f32[2,2,8,1,1536]{4,2,3,1,0:T(8,128)S(1)}, f32[2,2,8,1,1536]{4,2,3,1,0:T(8,128)S(1)}, u32[]{:S(2)}, u32[]{:S(2)}) collective-permute-start(f32[2,2,8,1,1536]{4,2,3,1,0:T(8,128)S(1)} %get-tuple-element.113), channel_id=1, source_target_pairs={{0,1},{1,2},{2,3},{3,4},{4,5},{5,6},{6,7},{7,8},{8,9},{9,10},{10,1... | collective-permute-start | bytes 589832 | tf_op jit(solution)/shard_map/ppermute | solution.py:21
  114.4 2.6 copy-start.3
  118.7 5.2 %copy-start.11 = (f32[2,1,192]{2,1,0:T(1,128)S(1)}, f32[2,1,192]{2,1,0:T(1,128)}, u32[]{:S(2)}) copy-start(f32[2,1,192]{2,1,0:T(1,128)} %copy.70) | copy-start | bytes 4612
  118.7 11.1 %copy-start.15 = (f32[2]{0:T(128)S(1)}, f32[2]{0:T(128)}, u32[]{:S(2)}) copy-start(f32[2]{0:T(128)} %multiply_reduce_fusion) | copy-start | bytes 28
  118.8 5.1 %collective-permute-start.4 = (f32[2,2,8,1,1536]{4,2,3,1,0:T(8,128)S(1)}, f32[2,2,8,1,1536]{4,2,3,1,0:T(8,128)S(1)}, u32[]{:S(2)}, u32[]{:S(2)}) collective-permute-start(f32[2,2,8,1,1536]{4,2,3,1,0:T(8,128)S(1)} %get-tuple-element.106), channel_id=1, source_target_pairs={{1,0},{2,1},{3,2},{4,3},{5,4},{6,5},{7,6},{8,7},{9,8},{10,9},{11,1... | collective-permute-start | bytes 589832 | tf_op jit(solution)/shard_map/ppermute | solution.py:24
  120.7 9.1 %collective-permute-start.5 = (f32[2,2,8,1,1536]{4,2,3,1,0:T(8,128)S(1)}, f32[2,2,8,1,1536]{4,2,3,1,0:T(8,128)S(1)}, u32[]{:S(2)}, u32[]{:S(2)}) collective-permute-start(f32[2,2,8,1,1536]{4,2,3,1,0:T(8,128)S(1)} %get-tuple-element.107), channel_id=1, source_target_pairs={{0,1},{1,2},{2,3},{3,4},{4,5},{5,6},{6,7},{7,8},{8,9},{9,10},{10,1... | collective-permute-start | bytes 589832 | tf_op jit(solution)/shard_map/ppermute | solution.py:21
  123.9 104.1 %collective-permute-start.9 = (f32[2,1,192]{2,1,0:T(1,128)S(1)}, f32[2,1,192]{2,1,0:T(1,128)S(1)}, u32[]{:S(2)}, u32[]{:S(2)}) collective-permute-start(f32[2,1,192]{2,1,0:T(1,128)S(1)} %copy-done.11), channel_id=1, source_target_pairs={{0,1},{1,2},{2,3},{3,4},{4,5},{5,6},{6,7},{7,8},{8,9},{9,10},{10,1... | collective-permute-start | bytes 4616 | tf_op jit(solution)/shard_map/ppermute | solution.py:21
  129.8 2.6 copy-start.4
  140.1 87.9 %copy-start.7 = (f32[2,6,192]{2,1,0:T(8,128)S(1)}, f32[2,6,192]{2,1,0:T(8,128)}, u32[]{:S(2)}) copy-start(f32[2,6,192]{2,1,0:T(8,128)} %copy-done.6) | copy-start | bytes 27652
  140.1 87.9 %copy-start.8 = (f32[6,192]{1,0:T(8,128)S(1)}, f32[6,192]{1,0:T(8,128)}, u32[]{:S(2)}) copy-start(f32[6,192]{1,0:T(8,128)} %param.21) | copy-start | bytes 13828
  140.1 299.0 %reduce-scatter.9.cloned.1.call-start = ((), (), s32[]{:S(2)}) async-start(), calls=%async_computation.3 | async-start | bytes 884736
  140.9 172.3 %collective-permute-start.6 = (f32[2,2,8,1,1536]{4,2,3,1,0:T(8,128)}, f32[2,2,8,1,1536]{4,2,3,1,0:T(8,128)}, u32[]{:S(2)}, u32[]{:S(2)}) collective-permute-start(f32[2,2,8,1,1536]{4,2,3,1,0:T(8,128)} %get-tuple-element.100), channel_id=1, source_target_pairs={{1,0},{2,1},{3,2},{4,3},{5,4},{6,5},{7,6},{8,7},{9,8},{10,9},{11,1... | collective-permute-start | bytes 589832 | tf_op jit(solution)/shard_map/ppermute | solution.py:24
  226.0 87.2 %collective-permute-start.7 = (f32[2,2,8,1,1536]{4,2,3,1,0:T(8,128)}, f32[2,2,8,1,1536]{4,2,3,1,0:T(8,128)}, u32[]{:S(2)}, u32[]{:S(2)}) collective-permute-start(f32[2,2,8,1,1536]{4,2,3,1,0:T(8,128)} %get-tuple-element.101), channel_id=1, source_target_pairs={{0,1},{1,2},{2,3},{3,4},{4,5},{5,6},{6,7},{7,8},{8,9},{9,10},{10,1... | collective-permute-start | bytes 589832 | tf_op jit(solution)/shard_map/ppermute | solution.py:21
  228.8 27.7 %collective-permute-start.12 = (f32[2,1,192]{2,1,0:T(1,128)S(1)}, f32[2,1,192]{2,1,0:T(1,128)S(1)}, u32[]{:S(2)}, u32[]{:S(2)}) collective-permute-start(f32[2,1,192]{2,1,0:T(1,128)S(1)} %get-tuple-element.128), channel_id=1, source_target_pairs={{1,0},{2,1},{3,2},{4,3},{5,4},{6,5},{7,6},{8,7},{9,8},{10,9},{11,1... | collective-permute-start | bytes 4616 | tf_op jit(solution)/shard_map/ppermute | solution.py:24
  234.6 21.9 %collective-permute-start.13 = (f32[2,1,192]{2,1,0:T(1,128)S(1)}, f32[2,1,192]{2,1,0:T(1,128)S(1)}, u32[]{:S(2)}, u32[]{:S(2)}) collective-permute-start(f32[2,1,192]{2,1,0:T(1,128)S(1)} %get-tuple-element.129), channel_id=1, source_target_pairs={{0,1},{1,2},{2,3},{3,4},{4,5},{5,6},{6,7},{7,8},{8,9},{9,10},{10,1... | collective-permute-start | bytes 4616 | tf_op jit(solution)/shard_map/ppermute | solution.py:21
  236.6 7.9 %collective-permute-start.14 = (f32[2,6,1]{2,1,0:T(8,128)S(1)}, f32[2,6,1]{2,1,0:T(8,128)S(1)}, u32[]{:S(2)}, u32[]{:S(2)}) collective-permute-start(f32[2,6,1]{2,1,0:T(8,128)S(1)} %get-tuple-element.130), channel_id=1, source_target_pairs={{64,0},{128,64},{192,128},{256,192},{320,256},{384,320},{448,384},... | collective-permute-start | bytes 152 | tf_op jit(solution)/shard_map/ppermute | solution.py:24
  244.5 12.0 %collective-permute-start.15 = (f32[2,6,1]{2,1,0:T(8,128)S(1)}, f32[2,6,1]{2,1,0:T(8,128)S(1)}, u32[]{:S(2)}, u32[]{:S(2)}) collective-permute-start(f32[2,6,1]{2,1,0:T(8,128)S(1)} %get-tuple-element.131), channel_id=1, source_target_pairs={{0,64},{64,128},{128,192},{192,256},{256,320},{320,384},{384,448},... | collective-permute-start | bytes 152 | tf_op jit(solution)/shard_map/ppermute | solution.py:21
  308.1 5.1 %copy-start.5 = (f32[2,8,6,1536]{3,1,2,0:T(8,128)S(1)}, f32[2,8,6,1536]{3,1,2,0:T(8,128)}, u32[]{:S(2)}) copy-start(f32[2,8,6,1536]{3,1,2,0:T(8,128)} %fusion.98) | copy-start | bytes 1769476
  308.1 5.1 %copy-start.16 = (f32[2]{0:T(128)S(1)}, f32[2]{0:T(128)}, u32[]{:S(2)}) copy-start(f32[2]{0:T(128)} %multiply_reduce_fusion) | copy-start | bytes 28
  308.8 131.5 %collective-permute-start.20 = (f32[2,1,192]{2,1,0:T(1,128)S(1)}, f32[2,1,192]{2,1,0:T(1,128)S(1)}, u32[]{:S(2)}, u32[]{:S(2)}) collective-permute-start(f32[2,1,192]{2,1,0:T(1,128)S(1)} %get-tuple-element.124), channel_id=1, source_target_pairs={{1,0},{2,1},{3,2},{4,3},{5,4},{6,5},{7,6},{8,7},{9,8},{10,9},{11,1... | collective-permute-start | bytes 4616 | tf_op jit(solution)/shard_map/ppermute | solution.py:24
  310.8 129.6 %collective-permute-start.21 = (f32[2,1,192]{2,1,0:T(1,128)S(1)}, f32[2,1,192]{2,1,0:T(1,128)S(1)}, u32[]{:S(2)}, u32[]{:S(2)}) collective-permute-start(f32[2,1,192]{2,1,0:T(1,128)S(1)} %get-tuple-element.125), channel_id=1, source_target_pairs={{0,1},{1,2},{2,3},{3,4},{4,5},{5,6},{6,7},{7,8},{8,9},{9,10},{10,1... | collective-permute-start | bytes 4616 | tf_op jit(solution)/shard_map/ppermute | solution.py:21
  320.1 8.4 %collective-permute-start.16 = (f32[2,2,8,1,1536]{4,2,3,1,0:T(8,128)S(1)}, f32[2,2,8,1,1536]{4,2,3,1,0:T(8,128)S(1)}, u32[]{:S(2)}, u32[]{:S(2)}) collective-permute-start(f32[2,2,8,1,1536]{4,2,3,1,0:T(8,128)S(1)} %get-tuple-element.92), channel_id=1, source_target_pairs={{1,0},{2,1},{3,2},{4,3},{5,4},{6,5},{7,6},{8,7},{9,8},{10,9},{11,1... | collective-permute-start | bytes 589832 | tf_op jit(solution)/shard_map/ppermute | solution.py:24
  325.4 9.1 %collective-permute-start.17 = (f32[2,2,8,1,1536]{4,2,3,1,0:T(8,128)S(1)}, f32[2,2,8,1,1536]{4,2,3,1,0:T(8,128)S(1)}, u32[]{:S(2)}, u32[]{:S(2)}) collective-permute-start(f32[2,2,8,1,1536]{4,2,3,1,0:T(8,128)S(1)} %get-tuple-element.93), channel_id=1, source_target_pairs={{0,1},{1,2},{2,3},{3,4},{4,5},{5,6},{6,7},{7,8},{8,9},{9,10},{10,1... | collective-permute-start | bytes 589832 | tf_op jit(solution)/shard_map/ppermute | solution.py:21
  338.8 5.1 %collective-permute-start.18 = (f32[2,2,8,1,1536]{4,2,3,1,0:T(8,128)S(1)}, f32[2,2,8,1,1536]{4,2,3,1,0:T(8,128)S(1)}, u32[]{:S(2)}, u32[]{:S(2)}) collective-permute-start(f32[2,2,8,1,1536]{4,2,3,1,0:T(8,128)S(1)} %get-tuple-element.86), channel_id=1, source_target_pairs={{1,0},{2,1},{3,2},{4,3},{5,4},{6,5},{7,6},{8,7},{9,8},{10,9},{11,1... | collective-permute-start | bytes 589832 | tf_op jit(solution)/shard_map/ppermute | solution.py:24
  340.7 9.1 %collective-permute-start.19 = (f32[2,2,8,1,1536]{4,2,3,1,0:T(8,128)S(1)}, f32[2,2,8,1,1536]{4,2,3,1,0:T(8,128)S(1)}, u32[]{:S(2)}, u32[]{:S(2)}) collective-permute-start(f32[2,2,8,1,1536]{4,2,3,1,0:T(8,128)S(1)} %get-tuple-element.87), channel_id=1, source_target_pairs={{0,1},{1,2},{2,3},{3,4},{4,5},{5,6},{6,7},{7,8},{8,9},{9,10},{10,1... | collective-permute-start | bytes 589832 | tf_op jit(solution)/shard_map/ppermute | solution.py:21
  355.9 84.4 %collective-permute-start.22 = (f32[2,6,1]{2,1,0:T(8,128)S(1)}, f32[2,6,1]{2,1,0:T(8,128)S(1)}, u32[]{:S(2)}, u32[]{:S(2)}) collective-permute-start(f32[2,6,1]{2,1,0:T(8,128)S(1)} %get-tuple-element.126), channel_id=1, source_target_pairs={{64,0},{128,64},{192,128},{256,192},{320,256},{384,320},{448,384},... | collective-permute-start | bytes 152 | tf_op jit(solution)/shard_map/ppermute | solution.py:24
  357.8 82.5 %collective-permute-start.23 = (f32[2,6,1]{2,1,0:T(8,128)S(1)}, f32[2,6,1]{2,1,0:T(8,128)S(1)}, u32[]{:S(2)}, u32[]{:S(2)}) collective-permute-start(f32[2,6,1]{2,1,0:T(8,128)S(1)} %get-tuple-element.127), channel_id=1, source_target_pairs={{0,64},{64,128},{128,192},{192,256},{256,320},{320,384},{384,448},... | collective-permute-start | bytes 152 | tf_op jit(solution)/shard_map/ppermute | solution.py:21
  362.6 103.6 %copy-start.10 = (f32[2,2,8,6,1536]{4,2,3,1,0:T(8,128)}, f32[2,2,8,6,1536]{4,2,3,1,0:T(8,128)S(1)}, u32[]{:S(2)}) copy-start(f32[2,2,8,6,1536]{4,2,3,1,0:T(8,128)S(1)} %scatter.29) | copy-start | bytes 3538948
  440.4 25.0 %collective-permute-start.24 = (f32[2,1,192]{2,1,0:T(1,128)S(1)}, f32[2,1,192]{2,1,0:T(1,128)S(1)}, u32[]{:S(2)}, u32[]{:S(2)}) collective-permute-start(f32[2,1,192]{2,1,0:T(1,128)S(1)} %get-tuple-element.120), channel_id=1, source_target_pairs={{1,0},{2,1},{3,2},{4,3},{5,4},{6,5},{7,6},{8,7},{9,8},{10,9},{11,1... | collective-permute-start | bytes 4616 | tf_op jit(solution)/shard_map/ppermute | solution.py:24
  443.9 21.6 %collective-permute-start.25 = (f32[2,1,192]{2,1,0:T(1,128)S(1)}, f32[2,1,192]{2,1,0:T(1,128)S(1)}, u32[]{:S(2)}, u32[]{:S(2)}) collective-permute-start(f32[2,1,192]{2,1,0:T(1,128)S(1)} %get-tuple-element.121), channel_id=1, source_target_pairs={{0,1},{1,2},{2,3},{3,4},{4,5},{5,6},{6,7},{7,8},{8,9},{9,10},{10,1... | collective-permute-start | bytes 4616 | tf_op jit(solution)/shard_map/ppermute | solution.py:21
  445.9 9.9 %collective-permute-start.26 = (f32[2,6,1]{2,1,0:T(8,128)S(1)}, f32[2,6,1]{2,1,0:T(8,128)S(1)}, u32[]{:S(2)}, u32[]{:S(2)}) collective-permute-start(f32[2,6,1]{2,1,0:T(8,128)S(1)} %get-tuple-element.122), channel_id=1, source_target_pairs={{64,0},{128,64},{192,128},{256,192},{320,256},{384,320},{448,384},... | collective-permute-start | bytes 152 | tf_op jit(solution)/shard_map/ppermute | solution.py:24
  453.9 11.6 %collective-permute-start.27 = (f32[2,6,1]{2,1,0:T(8,128)S(1)}, f32[2,6,1]{2,1,0:T(8,128)S(1)}, u32[]{:S(2)}, u32[]{:S(2)}) collective-permute-start(f32[2,6,1]{2,1,0:T(8,128)S(1)} %get-tuple-element.123), channel_id=1, source_target_pairs={{0,64},{64,128},{128,192},{192,256},{256,320},{320,384},{384,448},... | collective-permute-start | bytes 152 | tf_op jit(solution)/shard_map/ppermute | solution.py:21
Sparse Core Ops, SparseCore 0:
  140.2 84.5 reduce-scatter.6
  355.9 83.1 reduce-scatter.8
where the time goes:
time: 474 us; the launch traced here: 473 us
  waiting for transfers between devices  204 us (43%)
  blocking collectives  102 us (22%)
  starting transfers between devices  93.5 us (20%)
  local copies, waits for them, and re-layouts  29.9 us (6%)
  matrix products  21.1 us (4%)
  between operations  14.8 us (3%)
  other arithmetic  7.27 us (2%)
    unnamed x4, waiting for transfers between devices  159 us
    all_gather x2, blocking collectives, body(): surface = lax.all_gather(ocean, 'member', axis=2, tiled=True)  102 us
    ppermute x14, starting transfers between devices, with_halo(): lax.ppermute(lax.slice_in_dim(block, 0, width, axis=dim), axis, backward)  62.5 us
    ppermute x14, waiting for transfers between devices, with_halo(): lax.ppermute(lax.slice_in_dim(block, block.shape[dim] - width, None, axis...  41.4 us
    ppermute x14, starting transfers between devices, with_halo(): lax.ppermute(lax.slice_in_dim(block, block.shape[dim] - width, None, axis...  31 us
    dot_general x6, matrix products, atmos_step(): jnp.einsum('kl,fmlrn->fmkrn', level_mix, advected, precision=lax.Precisio...  20.9 us
  transfers between devices with their start and end apart: 30, of which 13 were waited for; matrix products, arithmetic and copies ran while one was open for 12% of the time, Pallas kernels for 0%

commit v1 on v0

--- a/solution.py
+++ b/solution.py
@@ -86,7 +86,9 @@
     ocean_rate = jnp.stack([jnp.full_like(viscosity, OCEAN_DIFFUSION), viscosity])
     atmos_state = atmosphere
     for coupling in range(COUPLE):
-        surface = lax.all_gather(ocean, "member", axis=2, tiled=True)
+        surface = jnp.concatenate(
+            lax.all_to_all(jnp.stack([ocean] * lax.axis_size("member")), "member", 0, 0), axis=2
+        )
         atmos_state = atmos_window(atmos_state, surface, diffusivity, exchange, level_mix)
         flux_terms = jnp.sum(
             exchange[:, :, None, None] * (atmos_state[:, :, 0] - surface[:, None]), axis=1

time: 474 us -> 397 us (0.84)
  blocking collectives: 102 us -> 0 us
  starting transfers between devices: 93.5 us -> 112 us
  waiting for transfers between devices: 204 us -> 209 us
    all_gather x2 -> x0, blocking collectives: 102 us -> none  [body(): surface = lax.all_gather(ocean, 'member', axis=2, tiled=True)]
    all_to_all x0 -> x2, starting transfers between devices: none -> 16.9 us  [body(): lax.all_to_all(jnp.stack([ocean] * lax.axis_size('member')), 'member', 0, 0)]
    unnamed x4, waiting for transfers between devices: 159 us -> 163 us
    unnamed x45 -> x58, local copies, waits for them, and re-layouts: 9.13 us -> 10.5 us
  transfers between devices with their start and end apart: 30 -> 32, of which waited for: 13 -> 13; matrix products, arithmetic and copies ran while one was open for 12% -> 14% of each run, Pallas kernels for 0% -> 0%
where the time goes in v1:
time: 397 us; the launch traced here: 396 us
  waiting for transfers between devices  209 us (53%)
  starting transfers between devices  112 us (28%)
  local copies, waits for them, and re-layouts  32.3 us (8%)
  matrix products  20.7 us (5%)
  between operations  14.9 us (4%)
  other arithmetic  7.05 us (2%)
    unnamed x4, waiting for transfers between devices  163 us
    ppermute x14, starting transfers between devices, with_halo(): lax.ppermute(lax.slice_in_dim(block, 0, width, axis=dim), axis, backward)  66.2 us
    ppermute x14, waiting for transfers between devices, with_halo(): lax.ppermute(lax.slice_in_dim(block, block.shape[dim] - width, None, axis...  41.2 us
    ppermute x14, starting transfers between devices, with_halo(): lax.ppermute(lax.slice_in_dim(block, block.shape[dim] - width, None, axis...  28.5 us
    dot_general x6, matrix products, atmos_step(): jnp.einsum('kl,fmlrn->fmkrn', level_mix, advected, precision=lax.Precisio...  20.5 us
    all_to_all x2, starting transfers between devices, body(): lax.all_to_all(jnp.stack([ocean] * lax.axis_size('member')), 'member', 0, 0)  16.9 us
    unnamed x58, local copies, waits for them, and re-layouts  10.5 us
    slice x12, local copies, waits for them, and re-layouts, atmos_step(): eastern = jnp.roll(centre, -1, axis=4)  8.78 us
  transfers between devices with their start and end apart: 32, of which 13 were waited for; matrix products, arithmetic and copies ran while one was open for 14% of the time, Pallas kernels for 0%

profile of v1, /device:TPU:48, one launch (start us, length us, event | category | flops | bytes accessed | tf_op | source)
XLA Modules:
  0.0 395.7 jit_solution(9996873179359695686)
XLA Ops:
  7.2 1.1 fusion.208
  8.2 11.2 %collective-permute-start = (f32[2,2,8,1,1536]{4,2,3,1,0:T(8,128)S(1)}, f32[2,2,8,1,1536]{4,2,3,1,0:T(8,128)S(1)}, u32[]{:S(2)}, u32[]{:S(2)}) collective-permute-start(f32[2,2,8,1,1536]{4,2,3,1,0:T(8,128)S(1)} %get-tuple-element.118), channel_id=1, source_target_pairs={{1,0},{2,1},{3,2},{4,3},{5,4},{6,5},{7,6},{8,7},{9,8},{10,9},{11,1... | collective-permute-start | bytes 589832 | tf_op jit(solution)/shard_map/ppermute | solution.py:24
  19.4 1.9 collective-permute-start.1
  21.3 1.4 stack.8
  22.7 9.7 %all-to-all-start = ((f32[8,2,6,192]{3,1,2,0:T(2,128)}), f32[8,2,6,192]{3,1,2,0:T(2,128)S(1)}, u32[]{:S(2)}, u32[]{:S(2)}) async-start(f32[8,2,6,192]{3,1,2,0:T(2,128)} %stack.8), calls=%async_computation | async-start | bytes 196608 | tf_op jit(solution)/shard_map/all_to_all | solution.py:90
  33.8 4.6 %collective-permute-start.10 = (f32[2,6,1]{2,1,0:T(8,128)}, f32[2,6,1]{2,1,0:T(8,128)}, u32[]{:S(2)}, u32[]{:S(2)}) collective-permute-start(f32[2,6,1]{2,1,0:T(8,128)} %get-tuple-element.132), channel_id=1, source_target_pairs={{64,0},{128,64},{192,128},{256,192},{320,256},{384,320},{448,384},... | collective-permute-start | bytes 152 | tf_op jit(solution)/shard_map/ppermute | solution.py:24
  38.3 1.9 collective-permute-start.11
  41.6 5.0 %collective-permute-start.8 = (f32[2,1,192]{2,1,0:T(1,128)}, f32[2,1,192]{2,1,0:T(1,128)}, u32[]{:S(2)}, u32[]{:S(2)}) collective-permute-start(f32[2,1,192]{2,1,0:T(1,128)} %copy.72), channel_id=1, source_target_pairs={{1,0},{2,1},{3,2},{4,3},{5,4},{6,5},{7,6},{8,7},{9,8},{10,9},{11,1... | collective-permute-start | bytes 4616 | tf_op jit(solution)/shard_map/ppermute | solution.py:24
  46.6 3.5 fusion.206
  54.2 5.3 %fusion.5 = f32[2,2,8,6,1536]{4,2,3,1,0:T(8,128)S(1)} fusion(f32[2,2,8,6,1536]{4,2,3,1,0:T(8,128)S(1)} %copy-done.1, f32[2,2,8,1,1536]{4,2,3,1,0:T(8,128)} %copy-done.17, f32[2,2,8,1,1536]{4,2,3,1,0:T(8,128)} %copy-done.16, f32[2,2,8,6,1535]{4,2,3,1,0:T(8,128)} %get-tuple-element.115, f32[2,2,8,6,1]{4,2,3,1,0:T(8,128)} %get-tuple-element.117, ...), kind=kOutput, calls=%fused_computation.11 | convolution fusion | flops 37453824 | bytes 5701896 | tf_op jit(solution)/shard_map/kl,fmlrn->fmkrn/dot_general | solution.py:52
  59.8 0.9 scatter.20
  61.2 1.9 collective-permute-start.2
  63.2 2.4 collective-permute-start.3
  66.3 5.9 %collective-permute-done.3 = f32[2,2,8,1,1536]{4,2,3,1,0:T(8,128)S(1)} collective-permute-done((f32[2,2,8,1,1536]{4,2,3,1,0:T(8,128)S(1)}, f32[2,2,8,1,1536]{4,2,3,1,0:T(8,128)S(1)}, u32[]{:S(2)}, u32[]{:S(2)}) %collective-permute-start.3) | collective-permute-done | bytes 196640 | tf_op jit(solution)/shard_map/ppermute | solution.py:21
  72.3 2.6 fusion.4
  75.2 0.9 scatter.21
  76.6 1.9 collective-permute-start.4
  78.6 2.4 collective-permute-start.5
  81.7 1.9 collective-permute-start.9
  83.6 4.0 %collective-permute-done.5 = f32[2,2,8,1,1536]{4,2,3,1,0:T(8,128)S(1)} collective-permute-done((f32[2,2,8,1,1536]{4,2,3,1,0:T(8,128)S(1)}, f32[2,2,8,1,1536]{4,2,3,1,0:T(8,128)S(1)}, u32[]{:S(2)}, u32[]{:S(2)}) %collective-permute-start.5) | collective-permute-done | bytes 196640 | tf_op jit(solution)/shard_map/ppermute | solution.py:21
  87.7 2.6 fusion.3
  90.6 0.9 scatter.24
  91.5 1.8 fusion.197
  93.3 0.9 fusion.98
  94.6 0.8 copy.89
  95.4 1.8 reshape.267
  97.9 1.9 collective-permute-start.6
  99.9 85.8 %reduce-scatter.7.cloned.1.call-done = f32[192,12]{1,0:T(8,128)} async-done(((f32[1536,12]{1,0:T(8,128)}), f32[192,12]{1,0:T(8,128)}) %reduce-scatter.7.cloned.1.call-update) | async-done | bytes 9232
  185.6 1.0 reshape.268
  186.8 1.9 collective-permute-start.7
  189.6 5.8 %collective-permute-start.12 = (f32[2,1,192]{2,1,0:T(1,128)S(1)}, f32[2,1,192]{2,1,0:T(1,128)S(1)}, u32[]{:S(2)}, u32[]{:S(2)}) collective-permute-start(f32[2,1,192]{2,1,0:T(1,128)S(1)} %get-tuple-element.128), channel_id=1, source_target_pairs={{1,0},{2,1},{3,2},{4,3},{5,4},{6,5},{7,6},{8,7},{9,8},{10,9},{11,1... | collective-permute-start | bytes 4616 | tf_op jit(solution)/shard_map/ppermute | solution.py:24
  195.4 1.9 collective-permute-start.13
  197.4 6.6 %collective-permute-start.14 = (f32[2,6,1]{2,1,0:T(8,128)S(1)}, f32[2,6,1]{2,1,0:T(8,128)S(1)}, u32[]{:S(2)}, u32[]{:S(2)}) collective-permute-start(f32[2,6,1]{2,1,0:T(8,128)S(1)} %get-tuple-element.130), channel_id=1, source_target_pairs={{64,0},{128,64},{192,128},{256,192},{320,256},{384,320},{448,384},... | collective-permute-start | bytes 152 | tf_op jit(solution)/shard_map/ppermute | solution.py:24
  204.0 1.3 collective-permute-done.14
  205.3 2.1 collective-permute-start.15
  207.4 9.7 %collective-permute-done.15 = f32[2,6,1]{2,1,0:T(8,128)S(1)} collective-permute-done((f32[2,6,1]{2,1,0:T(8,128)S(1)}, f32[2,6,1]{2,1,0:T(8,128)S(1)}, u32[]{:S(2)}, u32[]{:S(2)}) %collective-permute-start.15) | collective-permute-done | bytes 80 | tf_op jit(solution)/shard_map/ppermute | solution.py:21
  217.9 7.2 %all-to-all-start.1 = ((f32[8,2,6,192]{3,1,2,0:T(2,128)}), f32[8,2,6,192]{3,1,2,0:T(2,128)}, u32[]{:S(2)}, u32[]{:S(2)}) async-start(f32[8,2,6,192]{3,1,2,0:T(2,128)} %stack.11), calls=%async_computation.1 | async-start | bytes 196608 | tf_op jit(solution)/shard_map/all_to_all | solution.py:90
  225.7 3.6 collective-permute-start.20
  229.3 1.9 collective-permute-start.21
  232.0 4.9 %fusion.2 = f32[2,2,8,6,1536]{4,2,3,1,0:T(8,128)S(1)} fusion(f32[2,2,8,6,1536]{4,2,3,1,0:T(8,128)S(1)} %scatter.24, f32[2,2,8,1,1536]{4,2,3,1,0:T(8,128)} %copy-done.15, f32[2,2,8,1,1536]{4,2,3,1,0:T(8,128)} %copy-done.14, f32[2,2,8,6,1535]{4,2,3,1,0:T(8,128)} %get-tuple-element.97, f32[2,2,8,6,1]{4,2,3,1,0:T(8,128)} %get-tuple-element.99, ...), kind=kOutput, calls=%fused_computation.5 | convolution fusion | flops 37453824 | bytes 5701896 | tf_op jit(solution)/shard_map/kl,fmlrn->fmkrn/dot_general | solution.py:52
  236.9 0.9 copy.95
  238.2 0.9 scatter.25
  239.7 5.8 %collective-permute-start.16 = (f32[2,2,8,1,1536]{4,2,3,1,0:T(8,128)S(1)}, f32[2,2,8,1,1536]{4,2,3,1,0:T(8,128)S(1)}, u32[]{:S(2)}, u32[]{:S(2)}) collective-permute-start(f32[2,2,8,1,1536]{4,2,3,1,0:T(8,128)S(1)} %get-tuple-element.92), channel_id=1, source_target_pairs={{1,0},{2,1},{3,2},{4,3},{5,4},{6,5},{7,6},{8,7},{9,8},{10,9},{11,1... | collective-permute-start | bytes 589832 | tf_op jit(solution)/shard_map/ppermute | solution.py:24
  245.4 1.9 collective-permute-start.17
  247.4 1.1 collective-permute-done.16
  248.6 5.9 %collective-permute-done.17 = f32[2,2,8,1,1536]{4,2,3,1,0:T(8,128)S(1)} collective-permute-done((f32[2,2,8,1,1536]{4,2,3,1,0:T(8,128)S(1)}, f32[2,2,8,1,1536]{4,2,3,1,0:T(8,128)S(1)}, u32[]{:S(2)}, u32[]{:S(2)}) %collective-permute-start.17) | collective-permute-done | bytes 196640 | tf_op jit(solution)/shard_map/ppermute | solution.py:21
  254.5 2.6 fusion.1
  257.4 0.9 scatter.26
  258.9 1.9 collective-permute-start.18
  260.8 2.4 collective-permute-start.19
  264.0 5.9 %collective-permute-done.19 = f32[2,2,8,1,1536]{4,2,3,1,0:T(8,128)S(1)} collective-permute-done((f32[2,2,8,1,1536]{4,2,3,1,0:T(8,128)S(1)}, f32[2,2,8,1,1536]{4,2,3,1,0:T(8,128)S(1)}, u32[]{:S(2)}, u32[]{:S(2)}) %collective-permute-start.19) | collective-permute-done | bytes 196640 | tf_op jit(solution)/shard_map/ppermute | solution.py:21
  269.9 2.6 fusion
  273.2 0.8 copy.91
  274.1 1.8 reshape.269
  276.0 4.6 %collective-permute-start.22 = (f32[2,6,1]{2,1,0:T(8,128)S(1)}, f32[2,6,1]{2,1,0:T(8,128)S(1)}, u32[]{:S(2)}, u32[]{:S(2)}) collective-permute-start(f32[2,6,1]{2,1,0:T(8,128)S(1)} %get-tuple-element.126), channel_id=1, source_target_pairs={{64,0},{128,64},{192,128},{256,192},{320,256},{384,320},{448,384},... | collective-permute-start | bytes 152 | tf_op jit(solution)/shard_map/ppermute | solution.py:24
  280.5 1.9 collective-permute-start.23
  282.5 0.9 scatter.29
  283.4 77.7 %reduce-scatter.9.cloned.1.call-done = f32[192,12]{1,0:T(8,128)} async-done(((f32[1536,12]{1,0:T(8,128)}), f32[192,12]{1,0:T(8,128)}) %reduce-scatter.9.cloned.1.call-update) | async-done | bytes 9232
  361.0 1.0 reshape.270
  363.1 3.5 collective-permute-start.24
  366.6 1.9 collective-permute-start.25
  368.6 8.0 %collective-permute-start.26 = (f32[2,6,1]{2,1,0:T(8,128)S(1)}, f32[2,6,1]{2,1,0:T(8,128)S(1)}, u32[]{:S(2)}, u32[]{:S(2)}) collective-permute-start(f32[2,6,1]{2,1,0:T(8,128)S(1)} %get-tuple-element.122), channel_id=1, source_target_pairs={{64,0},{128,64},{192,128},{256,192},{320,256},{384,320},{448,384},... | collective-permute-start | bytes 152 | tf_op jit(solution)/shard_map/ppermute | solution.py:24
  376.6 1.9 collective-permute-start.27
  378.5 9.6 %collective-permute-done.27 = f32[2,6,1]{2,1,0:T(8,128)S(1)} collective-permute-done((f32[2,6,1]{2,1,0:T(8,128)S(1)}, f32[2,6,1]{2,1,0:T(8,128)S(1)}, u32[]{:S(2)}, u32[]{:S(2)}) %collective-permute-start.27) | collective-permute-done | bytes 80 | tf_op jit(solution)/shard_map/ppermute | solution.py:21
  (130 shorter events, 19.5 us)
Async XLA Ops:
  7.2 47.0 %copy-start = (f32[8,8]{1,0:T(8,128)S(1)}, f32[8,8]{1,0:T(8,128)}, u32[]{:S(2)}) copy-start(f32[8,8]{1,0:T(8,128)} %param.25) | copy-start | bytes 772
  8.2 45.2 %collective-permute-start = (f32[2,2,8,1,1536]{4,2,3,1,0:T(8,128)S(1)}, f32[2,2,8,1,1536]{4,2,3,1,0:T(8,128)S(1)}, u32[]{:S(2)}, u32[]{:S(2)}) collective-permute-start(f32[2,2,8,1,1536]{4,2,3,1,0:T(8,128)S(1)} %get-tuple-element.118), channel_id=1, source_target_pairs={{1,0},{2,1},{3,2},{4,3},{5,4},{6,5},{7,6},{8,7},{9,8},{10,9},{11,1... | collective-permute-start | bytes 589832 | tf_op jit(solution)/shard_map/ppermute | solution.py:24
  19.4 34.0 %collective-permute-start.1 = (f32[2,2,8,1,1536]{4,2,3,1,0:T(8,128)S(1)}, f32[2,2,8,1,1536]{4,2,3,1,0:T(8,128)S(1)}, u32[]{:S(2)}, u32[]{:S(2)}) collective-permute-start(f32[2,2,8,1,1536]{4,2,3,1,0:T(8,128)S(1)} %get-tuple-element.119), channel_id=1, source_target_pairs={{0,1},{1,2},{2,3},{3,4},{4,5},{5,6},{6,7},{7,8},{8,9},{9,10},{10,1... | collective-permute-start | bytes 589832 | tf_op jit(solution)/shard_map/ppermute | solution.py:21
  22.7 30.6 %all-to-all-start = ((f32[8,2,6,192]{3,1,2,0:T(2,128)}), f32[8,2,6,192]{3,1,2,0:T(2,128)S(1)}, u32[]{:S(2)}, u32[]{:S(2)}) async-start(f32[8,2,6,192]{3,1,2,0:T(2,128)} %stack.8), calls=%async_computation | async-start | bytes 196608 | tf_op jit(solution)/shard_map/all_to_all | solution.py:90
  32.4 153.3 %reduce-scatter.7.cloned.1.call-start = ((), (), s32[]{:S(2)}) async-start(), calls=%async_computation.4 | async-start | bytes 884736
  33.1 17.0 %copy-start.8 = (f32[2,6,192]{2,1,0:T(8,128)}, f32[2,6,192]{2,1,0:T(8,128)S(1)}, u32[]{:S(2)}) copy-start(f32[2,6,192]{2,1,0:T(8,128)S(1)} %copy.81) | copy-start | bytes 27652
  33.8 153.1 %collective-permute-start.10 = (f32[2,6,1]{2,1,0:T(8,128)}, f32[2,6,1]{2,1,0:T(8,128)}, u32[]{:S(2)}, u32[]{:S(2)}) collective-permute-start(f32[2,6,1]{2,1,0:T(8,128)} %get-tuple-element.132), channel_id=1, source_target_pairs={{64,0},{128,64},{192,128},{256,192},{320,256},{384,320},{448,384},... | collective-permute-start | bytes 152 | tf_op jit(solution)/shard_map/ppermute | solution.py:24
  38.3 150.4 %collective-permute-start.11 = (f32[2,6,1]{2,1,0:T(8,128)}, f32[2,6,1]{2,1,0:T(8,128)}, u32[]{:S(2)}, u32[]{:S(2)}) collective-permute-start(f32[2,6,1]{2,1,0:T(8,128)} %get-tuple-element.133), channel_id=1, source_target_pairs={{0,64},{64,128},{128,192},{192,256},{256,320},{320,384},{384,448},... | collective-permute-start | bytes 152 | tf_op jit(solution)/shard_map/ppermute | solution.py:21
  41.5 8.5 %copy-start.1 = (f32[2,2,8,6,1536]{4,2,3,1,0:T(8,128)S(1)}, f32[2,2,8,6,1536]{4,2,3,1,0:T(8,128)}, u32[]{:S(2)}) copy-start(f32[2,2,8,6,1536]{4,2,3,1,0:T(8,128)} %param.19) | copy-start | bytes 3538948
  41.6 147.2 %collective-permute-start.8 = (f32[2,1,192]{2,1,0:T(1,128)}, f32[2,1,192]{2,1,0:T(1,128)}, u32[]{:S(2)}, u32[]{:S(2)}) collective-permute-start(f32[2,1,192]{2,1,0:T(1,128)} %copy.72), channel_id=1, source_target_pairs={{1,0},{2,1},{3,2},{4,3},{5,4},{6,5},{7,6},{8,7},{9,8},{10,9},{11,1... | collective-permute-start | bytes 4616 | tf_op jit(solution)/shard_map/ppermute | solution.py:24
  50.1 0.8 copy-start.18
  50.1 0.8 copy-start.19
  53.4 6.1 %copy-start.2 = (f32[2,6,1536]{2,1,0:T(8,128)}, f32[2,6,1536]{2,1,0:T(8,128)S(1)}, u32[]{:S(2)}) copy-start(f32[2,6,1536]{2,1,0:T(8,128)S(1)} %reshape.271) | copy-start | bytes 221188
  53.4 0.7 copy-start.16
  53.4 0.8 copy-start.17
  61.1 11.1 %copy-start.20 = (f32[2]{0:T(128)S(1)}, f32[2]{0:T(128)}, u32[]{:S(2)}) copy-start(f32[2]{0:T(128)} %multiply_reduce_fusion) | copy-start | bytes 28
  61.2 5.1 %collective-permute-start.2 = (f32[2,2,8,1,1536]{4,2,3,1,0:T(8,128)S(1)}, f32[2,2,8,1,1536]{4,2,3,1,0:T(8,128)S(1)}, u32[]{:S(2)}, u32[]{:S(2)}) collective-permute-start(f32[2,2,8,1,1536]{4,2,3,1,0:T(8,128)S(1)} %get-tuple-element.112), channel_id=1, source_target_pairs={{1,0},{2,1},{3,2},{4,3},{5,4},{6,5},{7,6},{8,7},{9,8},{10,9},{11,1... | collective-permute-start | bytes 589832 | tf_op jit(solution)/shard_map/ppermute | solution.py:24
  63.2 9.1 %collective-permute-start.3 = (f32[2,2,8,1,1536]{4,2,3,1,0:T(8,128)S(1)}, f32[2,2,8,1,1536]{4,2,3,1,0:T(8,128)S(1)}, u32[]{:S(2)}, u32[]{:S(2)}) collective-permute-start(f32[2,2,8,1,1536]{4,2,3,1,0:T(8,128)S(1)} %get-tuple-element.113), channel_id=1, source_target_pairs={{0,1},{1,2},{2,3},{3,4},{4,5},{5,6},{6,7},{7,8},{8,9},{9,10},{10,1... | collective-permute-start | bytes 589832 | tf_op jit(solution)/shard_map/ppermute | solution.py:21
  72.3 2.6 copy-start.3
  76.5 5.2 %copy-start.13 = (f32[2,1,192]{2,1,0:T(1,128)S(1)}, f32[2,1,192]{2,1,0:T(1,128)}, u32[]{:S(2)}) copy-start(f32[2,1,192]{2,1,0:T(1,128)} %copy.74) | copy-start | bytes 4612
  76.5 11.1 %copy-start.21 = (f32[2]{0:T(128)S(1)}, f32[2]{0:T(128)}, u32[]{:S(2)}) copy-start(f32[2]{0:T(128)} %multiply_reduce_fusion) | copy-start | bytes 28
  76.6 5.1 %collective-permute-start.4 = (f32[2,2,8,1,1536]{4,2,3,1,0:T(8,128)S(1)}, f32[2,2,8,1,1536]{4,2,3,1,0:T(8,128)S(1)}, u32[]{:S(2)}, u32[]{:S(2)}) collective-permute-start(f32[2,2,8,1,1536]{4,2,3,1,0:T(8,128)S(1)} %get-tuple-element.106), channel_id=1, source_target_pairs={{1,0},{2,1},{3,2},{4,3},{5,4},{6,5},{7,6},{8,7},{9,8},{10,9},{11,1... | collective-permute-start | bytes 589832 | tf_op jit(solution)/shard_map/ppermute | solution.py:24
  78.6 9.1 %collective-permute-start.5 = (f32[2,2,8,1,1536]{4,2,3,1,0:T(8,128)S(1)}, f32[2,2,8,1,1536]{4,2,3,1,0:T(8,128)S(1)}, u32[]{:S(2)}, u32[]{:S(2)}) collective-permute-start(f32[2,2,8,1,1536]{4,2,3,1,0:T(8,128)S(1)} %get-tuple-element.107), channel_id=1, source_target_pairs={{0,1},{1,2},{2,3},{3,4},{4,5},{5,6},{6,7},{7,8},{8,9},{9,10},{10,1... | collective-permute-start | bytes 589832 | tf_op jit(solution)/shard_map/ppermute | solution.py:21
  81.7 107.1 %collective-permute-start.9 = (f32[2,1,192]{2,1,0:T(1,128)S(1)}, f32[2,1,192]{2,1,0:T(1,128)S(1)}, u32[]{:S(2)}, u32[]{:S(2)}) collective-permute-start(f32[2,1,192]{2,1,0:T(1,128)S(1)} %copy-done.13), channel_id=1, source_target_pairs={{0,1},{1,2},{2,3},{3,4},{4,5},{5,6},{6,7},{7,8},{8,9},{9,10},{10,1... | collective-permute-start | bytes 4616 | tf_op jit(solution)/shard_map/ppermute | solution.py:21
  87.7 2.6 copy-start.4
  97.2 91.6 %copy-start.9 = (f32[2,6,192]{2,1,0:T(8,128)S(1)}, f32[2,6,192]{2,1,0:T(8,128)}, u32[]{:S(2)}) copy-start(f32[2,6,192]{2,1,0:T(8,128)} %copy-done.8) | copy-start | bytes 27652
  97.2 91.6 %copy-start.10 = (f32[6,192]{1,0:T(8,128)S(1)}, f32[6,192]{1,0:T(8,128)}, u32[]{:S(2)}) copy-start(f32[6,192]{1,0:T(8,128)} %param.21) | copy-start | bytes 13828
  97.2 134.8 %copy-start.5 = (f32[2,2,8,6,1535]{4,2,3,1,0:T(8,128)S(1)}, f32[2,2,8,6,1535]{4,2,3,1,0:T(8,128)}, u32[]{:S(2)}) copy-start(f32[2,2,8,6,1535]{4,2,3,1,0:T(8,128)} %get-tuple-element.96) | copy-start | bytes 3536644
  97.9 133.3 %collective-permute-start.6 = (f32[2,2,8,1,1536]{4,2,3,1,0:T(8,128)S(1)}, f32[2,2,8,1,1536]{4,2,3,1,0:T(8,128)S(1)}, u32[]{:S(2)}, u32[]{:S(2)}) collective-permute-start(f32[2,2,8,1,1536]{4,2,3,1,0:T(8,128)S(1)} %get-tuple-element.100), channel_id=1, source_target_pairs={{1,0},{2,1},{3,2},{4,3},{5,4},{6,5},{7,6},{8,7},{9,8},{10,9},{11,1... | collective-permute-start | bytes 589832 | tf_op jit(solution)/shard_map/ppermute | solution.py:24
  186.8 44.5 %collective-permute-start.7 = (f32[2,2,8,1,1536]{4,2,3,1,0:T(8,128)S(1)}, f32[2,2,8,1,1536]{4,2,3,1,0:T(8,128)S(1)}, u32[]{:S(2)}, u32[]{:S(2)}) collective-permute-start(f32[2,2,8,1,1536]{4,2,3,1,0:T(8,128)S(1)} %get-tuple-element.101), channel_id=1, source_target_pairs={{0,1},{1,2},{2,3},{3,4},{4,5},{5,6},{6,7},{7,8},{8,9},{9,10},{10,1... | collective-permute-start | bytes 589832 | tf_op jit(solution)/shard_map/ppermute | solution.py:21
  189.6 27.5 %collective-permute-start.12 = (f32[2,1,192]{2,1,0:T(1,128)S(1)}, f32[2,1,192]{2,1,0:T(1,128)S(1)}, u32[]{:S(2)}, u32[]{:S(2)}) collective-permute-start(f32[2,1,192]{2,1,0:T(1,128)S(1)} %get-tuple-element.128), channel_id=1, source_target_pairs={{1,0},{2,1},{3,2},{4,3},{5,4},{6,5},{7,6},{8,7},{9,8},{10,9},{11,1... | collective-permute-start | bytes 4616 | tf_op jit(solution)/shard_map/ppermute | solution.py:24
  195.4 21.8 %collective-permute-start.13 = (f32[2,1,192]{2,1,0:T(1,128)S(1)}, f32[2,1,192]{2,1,0:T(1,128)S(1)}, u32[]{:S(2)}, u32[]{:S(2)}) collective-permute-start(f32[2,1,192]{2,1,0:T(1,128)S(1)} %get-tuple-element.129), channel_id=1, source_target_pairs={{0,1},{1,2},{2,3},{3,4},{4,5},{5,6},{6,7},{7,8},{8,9},{9,10},{10,1... | collective-permute-start | bytes 4616 | tf_op jit(solution)/shard_map/ppermute | solution.py:21
  197.4 7.9 %collective-permute-start.14 = (f32[2,6,1]{2,1,0:T(8,128)S(1)}, f32[2,6,1]{2,1,0:T(8,128)S(1)}, u32[]{:S(2)}, u32[]{:S(2)}) collective-permute-start(f32[2,6,1]{2,1,0:T(8,128)S(1)} %get-tuple-element.130), channel_id=1, source_target_pairs={{64,0},{128,64},{192,128},{256,192},{320,256},{384,320},{448,384},... | collective-permute-start | bytes 152 | tf_op jit(solution)/shard_map/ppermute | solution.py:24
  205.3 11.8 %collective-permute-start.15 = (f32[2,6,1]{2,1,0:T(8,128)S(1)}, f32[2,6,1]{2,1,0:T(8,128)S(1)}, u32[]{:S(2)}, u32[]{:S(2)}) collective-permute-start(f32[2,6,1]{2,1,0:T(8,128)S(1)} %get-tuple-element.131), channel_id=1, source_target_pairs={{0,64},{64,128},{128,192},{192,256},{256,320},{320,384},{384,448},... | collective-permute-start | bytes 152 | tf_op jit(solution)/shard_map/ppermute | solution.py:21
  217.2 14.1 %copy-start.6 = (f32[2,6,192]{2,1,0:T(8,128)}, f32[2,6,192]{2,1,0:T(8,128)S(1)}, u32[]{:S(2)}) copy-start(f32[2,6,192]{2,1,0:T(8,128)S(1)} %fusion.138) | copy-start | bytes 27652
  217.9 19.0 %all-to-all-start.1 = ((f32[8,2,6,192]{3,1,2,0:T(2,128)}), f32[8,2,6,192]{3,1,2,0:T(2,128)}, u32[]{:S(2)}, u32[]{:S(2)}) async-start(f32[8,2,6,192]{3,1,2,0:T(2,128)} %stack.11), calls=%async_computation.1 | async-start | bytes 196608 | tf_op jit(solution)/shard_map/all_to_all | solution.py:90
  225.1 135.9 %reduce-scatter.9.cloned.1.call-start = ((), (), s32[]{:S(2)}) async-start(), calls=%async_computation.5 | async-start | bytes 884736
  225.7 136.5 %collective-permute-start.20 = (f32[2,1,192]{2,1,0:T(1,128)}, f32[2,1,192]{2,1,0:T(1,128)}, u32[]{:S(2)}, u32[]{:S(2)}) collective-permute-start(f32[2,1,192]{2,1,0:T(1,128)} %get-tuple-element.124), channel_id=1, source_target_pairs={{1,0},{2,1},{3,2},{4,3},{5,4},{6,5},{7,6},{8,7},{9,8},{10,9},{11,1... | collective-permute-start | bytes 4616 | tf_op jit(solution)/shard_map/ppermute | solution.py:24
  229.3 132.9 %collective-permute-start.21 = (f32[2,1,192]{2,1,0:T(1,128)}, f32[2,1,192]{2,1,0:T(1,128)}, u32[]{:S(2)}, u32[]{:S(2)}) collective-permute-start(f32[2,1,192]{2,1,0:T(1,128)} %get-tuple-element.125), channel_id=1, source_target_pairs={{0,1},{1,2},{2,3},{3,4},{4,5},{5,6},{6,7},{7,8},{8,9},{9,10},{10,1... | collective-permute-start | bytes 4616 | tf_op jit(solution)/shard_map/ppermute | solution.py:21
  231.3 0.7 copy-start.14
  231.3 0.7 copy-start.15
  239.5 15.0 %copy-start.22 = (f32[2]{0:T(128)S(1)}, f32[2]{0:T(128)}, u32[]{:S(2)}) copy-start(f32[2]{0:T(128)} %multiply_reduce_fusion) | copy-start | bytes 28
  239.7 8.9 %collective-permute-start.16 = (f32[2,2,8,1,1536]{4,2,3,1,0:T(8,128)S(1)}, f32[2,2,8,1,1536]{4,2,3,1,0:T(8,128)S(1)}, u32[]{:S(2)}, u32[]{:S(2)}) collective-permute-start(f32[2,2,8,1,1536]{4,2,3,1,0:T(8,128)S(1)} %get-tuple-element.92), channel_id=1, source_target_pairs={{1,0},{2,1},{3,2},{4,3},{5,4},{6,5},{7,6},{8,7},{9,8},{10,9},{11,1... | collective-permute-start | bytes 589832 | tf_op jit(solution)/shard_map/ppermute | solution.py:24
  245.4 9.1 %collective-permute-start.17 = (f32[2,2,8,1,1536]{4,2,3,1,0:T(8,128)S(1)}, f32[2,2,8,1,1536]{4,2,3,1,0:T(8,128)S(1)}, u32[]{:S(2)}, u32[]{:S(2)}) collective-permute-start(f32[2,2,8,1,1536]{4,2,3,1,0:T(8,128)S(1)} %get-tuple-element.93), channel_id=1, source_target_pairs={{0,1},{1,2},{2,3},{3,4},{4,5},{5,6},{6,7},{7,8},{8,9},{9,10},{10,1... | collective-permute-start | bytes 589832 | tf_op jit(solution)/shard_map/ppermute | solution.py:21
  258.8 11.1 %copy-start.23 = (f32[2]{0:T(128)S(1)}, f32[2]{0:T(128)}, u32[]{:S(2)}) copy-start(f32[2]{0:T(128)} %multiply_reduce_fusion) | copy-start | bytes 28
  258.9 5.1 %collective-permute-start.18 = (f32[2,2,8,1,1536]{4,2,3,1,0:T(8,128)S(1)}, f32[2,2,8,1,1536]{4,2,3,1,0:T(8,128)S(1)}, u32[]{:S(2)}, u32[]{:S(2)}) collective-permute-start(f32[2,2,8,1,1536]{4,2,3,1,0:T(8,128)S(1)} %get-tuple-element.86), channel_id=1, source_target_pairs={{1,0},{2,1},{3,2},{4,3},{5,4},{6,5},{7,6},{8,7},{9,8},{10,9},{11,1... | collective-permute-start | bytes 589832 | tf_op jit(solution)/shard_map/ppermute | solution.py:24
  260.8 9.1 %collective-permute-start.19 = (f32[2,2,8,1,1536]{4,2,3,1,0:T(8,128)S(1)}, f32[2,2,8,1,1536]{4,2,3,1,0:T(8,128)S(1)}, u32[]{:S(2)}, u32[]{:S(2)}) collective-permute-start(f32[2,2,8,1,1536]{4,2,3,1,0:T(8,128)S(1)} %get-tuple-element.87), channel_id=1, source_target_pairs={{0,1},{1,2},{2,3},{3,4},{4,5},{5,6},{6,7},{7,8},{8,9},{9,10},{10,1... | collective-permute-start | bytes 589832 | tf_op jit(solution)/shard_map/ppermute | solution.py:21
  274.0 1.8 copy-start.7
  275.9 86.4 %copy-start.11 = (f32[6,192]{1,0:T(8,128)S(1)}, f32[6,192]{1,0:T(8,128)}, u32[]{:S(2)}) copy-start(f32[6,192]{1,0:T(8,128)} %param.21) | copy-start | bytes 13828
  276.0 86.3 %collective-permute-start.22 = (f32[2,6,1]{2,1,0:T(8,128)S(1)}, f32[2,6,1]{2,1,0:T(8,128)S(1)}, u32[]{:S(2)}, u32[]{:S(2)}) collective-permute-start(f32[2,6,1]{2,1,0:T(8,128)S(1)} %get-tuple-element.126), channel_id=1, source_target_pairs={{64,0},{128,64},{192,128},{256,192},{320,256},{384,320},{448,384},... | collective-permute-start | bytes 152 | tf_op jit(solution)/shard_map/ppermute | solution.py:24
  280.5 81.7 %collective-permute-start.23 = (f32[2,6,1]{2,1,0:T(8,128)S(1)}, f32[2,6,1]{2,1,0:T(8,128)S(1)}, u32[]{:S(2)}, u32[]{:S(2)}) collective-permute-start(f32[2,6,1]{2,1,0:T(8,128)S(1)} %get-tuple-element.127), channel_id=1, source_target_pairs={{0,64},{64,128},{128,192},{192,256},{256,320},{320,384},{384,448},... | collective-permute-start | bytes 152 | tf_op jit(solution)/shard_map/ppermute | solution.py:21
  283.4 105.5 %copy-start.12 = (f32[2,2,8,6,1536]{4,2,3,1,0:T(8,128)}, f32[2,2,8,6,1536]{4,2,3,1,0:T(8,128)S(1)}, u32[]{:S(2)}) copy-start(f32[2,2,8,6,1536]{4,2,3,1,0:T(8,128)S(1)} %scatter.29) | copy-start | bytes 3538948
  363.1 25.1 %collective-permute-start.24 = (f32[2,1,192]{2,1,0:T(1,128)S(1)}, f32[2,1,192]{2,1,0:T(1,128)S(1)}, u32[]{:S(2)}, u32[]{:S(2)}) collective-permute-start(f32[2,1,192]{2,1,0:T(1,128)S(1)} %get-tuple-element.120), channel_id=1, source_target_pairs={{1,0},{2,1},{3,2},{4,3},{5,4},{6,5},{7,6},{8,7},{9,8},{10,9},{11,1... | collective-permute-start | bytes 4616 | tf_op jit(solution)/shard_map/ppermute | solution.py:24
  366.6 21.6 %collective-permute-start.25 = (f32[2,1,192]{2,1,0:T(1,128)S(1)}, f32[2,1,192]{2,1,0:T(1,128)S(1)}, u32[]{:S(2)}, u32[]{:S(2)}) collective-permute-start(f32[2,1,192]{2,1,0:T(1,128)S(1)} %get-tuple-element.121), channel_id=1, source_target_pairs={{0,1},{1,2},{2,3},{3,4},{4,5},{5,6},{6,7},{7,8},{8,9},{9,10},{10,1... | collective-permute-start | bytes 4616 | tf_op jit(solution)/shard_map/ppermute | solution.py:21
  368.6 9.9 %collective-permute-start.26 = (f32[2,6,1]{2,1,0:T(8,128)S(1)}, f32[2,6,1]{2,1,0:T(8,128)S(1)}, u32[]{:S(2)}, u32[]{:S(2)}) collective-permute-start(f32[2,6,1]{2,1,0:T(8,128)S(1)} %get-tuple-element.122), channel_id=1, source_target_pairs={{64,0},{128,64},{192,128},{256,192},{320,256},{384,320},{448,384},... | collective-permute-start | bytes 152 | tf_op jit(solution)/shard_map/ppermute | solution.py:24
  376.6 11.6 %collective-permute-start.27 = (f32[2,6,1]{2,1,0:T(8,128)S(1)}, f32[2,6,1]{2,1,0:T(8,128)S(1)}, u32[]{:S(2)}, u32[]{:S(2)}) collective-permute-start(f32[2,6,1]{2,1,0:T(8,128)S(1)} %get-tuple-element.123), channel_id=1, source_target_pairs={{0,64},{64,128},{128,192},{192,256},{256,320},{320,384},{384,448},... | collective-permute-start | bytes 152 | tf_op jit(solution)/shard_map/ppermute | solution.py:21
Sparse Core Ops, SparseCore 0:
  97.3 88.2 reduce-scatter.6
  276.0 84.9 reduce-scatter.8
